TPU v7x, 32 devices: a whole 2x2x4 slice. The times are simulated.
32 devices in a mesh: shot: 8 (over z, y), rcv: 4 (over x, core).
Axes of the slice: x: 2, y: 2, z: 4, core: 2. Of those that a mesh axis runs over, the one named last changes fastest.
Arguments:
- data_matrix: bfloat16 [2, 16, 1024, 1024], P(None, None, 'shot', 'rcv'), may hold values from -12 to 12
- shot_records: bfloat16 [2, 16, 1024, 1024], P(None, None, 'rcv', 'shot'), may hold values from -4 to 4
- live: int32 [1024, 1024], P('rcv', 'shot'), may hold values 0 or 1
Outputs:
- predicted: bfloat16 [2, 16, 1024, 1024], P(None, None, 'rcv', 'shot')
- primaries: bfloat16 [2, 16, 1024, 1024], P(None, None, 'rcv', 'shot')
All inputs are finite; a program needn't handle non-finite values. No bound on the sum of `live` on one device may be relied on, other than what follows from the above.
Results may differ from a plain program's by a relative error of at most 0.013.
Values may be sent and summed in bfloat16 or wider, within the bound.
A program may use at most 128 MiB of HBM per device.

v0:
```python
import jax
import jax.numpy as jnp
from jax import lax
from jax.sharding import PartitionSpec as P


def complex_product(left, right):
    prod = jnp.einsum("afrk,bfks->abfrs", left, right, preferred_element_type=jnp.float32)
    return jnp.stack((prod[0, 0] - prod[1, 1], prod[0, 1] + prod[1, 0]))


def shards(data_matrix, shot_records, live):
    records = shot_records * live.astype(jnp.bfloat16)[None, None]
    own_rows = records.shape[2]
    partial_terms = complex_product(
        lax.all_gather(data_matrix, "shot", axis=2, tiled=True), records
    )
    summed = lax.psum(partial_terms.astype(jnp.bfloat16), "rcv").astype(jnp.float32)
    total = lax.dynamic_slice_in_dim(summed, lax.axis_index("rcv") * own_rows, own_rows, 2)
    rec = records.astype(jnp.float32)
    num_re = jnp.sum(total[0] * rec[0] + total[1] * rec[1], axis=1)
    num_im = jnp.sum(total[0] * rec[1] - total[1] * rec[0], axis=1)
    power = jnp.sum(total[0] * total[0] + total[1] * total[1], axis=1)
    sum_re, sum_im, sum_power = lax.psum((num_re, num_im, power), "rcv")
    points = float(own_rows * lax.axis_size("rcv"))
    power_mean = sum_power / points + 1e-06
    filt_re = (sum_re / points / power_mean)[:, None, :]
    filt_im = (sum_im / points / power_mean)[:, None, :]
    out_re = rec[0] - (filt_re * total[0] - filt_im * total[1])
    out_im = rec[1] - (filt_re * total[1] + filt_im * total[0])
    primaries = jnp.stack((out_re, out_im)).astype(jnp.bfloat16)
    return (total.astype(jnp.bfloat16), primaries)


def solution(mesh):
    in_specs = (P(None, None, "shot", "rcv"), P(None, None, "rcv", "shot"), P("rcv", "shot"))
    out_specs = (P(None, None, "rcv", "shot"), P(None, None, "rcv", "shot"))
    return jax.shard_map(shards, mesh=mesh, in_specs=in_specs, out_specs=out_specs, check_vma=False)
```

profile of v0, /device:TPU:0, one launch (start us, length us, event | category | flops | bytes accessed | tf_op | source)
XLA Modules:
  0.0 466.1 jit_solution(6643771911731964899)
XLA Ops:
  7.2 0.0 all-gather.2.cloned.1.call-start
  7.2 3.1 copy.7
  10.3 0.0 copy-start
  10.3 0.0 all-gather.2.cloned.1.call-update
  10.4 0.0 copy-start.1
  10.4 0.0 all-reduce.3.cloned.1.call-start
  10.4 1.5 copy-done
  11.9 2.6 copy.6
  14.5 0.0 copy-done.1
  14.5 0.1 copy.5
  14.6 4.0 multiply_convert_fusion
  18.7 222.4 %all-gather.2.cloned.1.call-done = bf16[2,16,1024,256]{3,2,0,1:T(8,128)(2,1)} async-done(((bf16[2,16,128,256]{3,2,0,1:T(8,128)(2,1)}), bf16[2,16,1024,256]{3,2,0,1:T(8,128)(2,1)}) %all-gather.2.cloned.1.call-update) | async-done | bytes 16777232 | tf_op jit(solution)/shard_map/all_gather | solution.py:16
  241.1 17.6 %fusion.2 = f32[2,2,16,1024,128]{3,4,0,1,2:T(8,128)} fusion(bf16[2,16,1024,256]{3,2,0,1:T(8,128)(2,1)} %all-gather.2.cloned.1.call-done, bf16[2,16,256,128,1]{2,3,1,0,4:T(8,128)(2,1)S(1)} %get-tuple-element.15), kind=kOutput, calls=%fused_computation.2 | convolution fusion | flops 4294967296 | bytes 52428800 | tf_op jit(solution)/shard_map/afrk,bfks->abfrs/dot_general | solution.py:8
  258.7 6.6 %fusion.9 = bf16[1,16,1024,128]{2,3,1,0:T(8,128)(2,1)S(1)} fusion(f32[2,2,16,1024,128]{3,4,0,1,2:T(8,128)} %fusion.2), kind=kLoop, calls=%fused_computation.11 | loop fusion | flops 4194304 | bytes 20971520 | tf_op jit(solution)/shard_map/add | solution.py:9
  265.3 8.8 %fusion.8 = bf16[1,16,1024,128]{2,3,1,0:T(8,128)(2,1)} fusion(f32[2,2,16,1024,128]{3,4,0,1,2:T(8,128)} %fusion.2), kind=kLoop, calls=%fused_computation.10 | loop fusion | flops 4194304 | bytes 20971520 | tf_op jit(solution)/shard_map/sub | solution.py:9
  274.0 6.2 %pad_maximum_fusion = bf16[2,16,1024,128]{2,3,1,0:T(8,128)(2,1)} fusion(bf16[1,16,1024,128]{2,3,1,0:T(8,128)(2,1)S(1)} %fusion.9, bf16[1,16,1024,128]{2,3,1,0:T(8,128)(2,1)} %fusion.8), kind=kLoop, calls=%fused_computation.9 | loop fusion | flops 4194304 | bytes 16777216 | tf_op jit(solution)/shard_map/stack | solution.py:9
  280.2 0.0 all-reduce.3.cloned.1.call-update
  280.2 151.2 %all-reduce.3.cloned.1.call-done = bf16[2,16,1024,128]{2,3,1,0:T(8,128)(2,1)} async-done(((bf16[2,16,1024,128]{2,3,1,0:T(8,128)(2,1)}), bf16[2,16,1024,128]{2,3,1,0:T(8,128)(2,1)}) %all-reduce.3.cloned.1.call-update) | async-done | bytes 8388624 | tf_op jit(solution)/shard_map/psum | solution.py:18
  431.4 4.1 dynamic-slice_convert_fusion
  435.5 2.4 copy.11
  437.9 4.6 add_reduce_fusion.1
  442.5 10.3 %all-reduce = (f32[16,128]{1,0:T(8,128)S(1)}, f32[16,128]{1,0:T(8,128)S(1)}, f32[16,128]{1,0:T(8,128)S(1)}) all-reduce(f32[16,128]{1,0:T(8,128)S(1)} %get-tuple-element.5, f32[16,128]{1,0:T(8,128)S(1)} %get-tuple-element.6, f32[16,128]{1,0:T(8,128)S(1)} %get-tuple-element.4), channel_id=1, replica_groups=mesh['shot'=8,'rcv'=4] {'rcv'}, use_global_device_ids=true, to_apply=%region_6.0 | all-reduce | flops 6144 | bytes 49152 | tf_op jit(solution)/shard_map/psum | solution.py:24
  452.8 3.8 subtract_convert_fusion.1
  456.7 0.2 pad_maximum_fusion.1
  456.9 2.4 copy.12
  (2 shorter events, 0.0 us)
Async XLA Ops:
  7.2 233.9 %all-gather.2.cloned.1.call-start = ((), (), s32[]{:S(2)}) async-start(), calls=%async_computation | async-start | bytes 18874368 | tf_op jit(solution)/shard_map/all_gather | solution.py:16
  10.3 1.6 copy-start
  10.4 4.1 copy-start.1
  10.4 421.0 %all-reduce.3.cloned.1.call-start = ((), (), s32[]{:S(2)}) async-start(), calls=%async_computation.1 | async-start | bytes 16777216 | tf_op jit(solution)/shard_map/psum | solution.py:18
Sparse Core Ops, SparseCore 0:
  10.8 230.2 all-gather.1
  280.4 151.0 all-reduce.2
where the time goes:
time: 466 us
  waiting for transfers between devices  374 us (80%)
  other arithmetic  38.4 us (8%)
  matrix products  17.6 us (4%)
  between operations  14.1 us (3%)
  local copies, waits for them, and re-layouts  12.1 us (3%)
  blocking collectives  10.3 us (2%)
    all_gather x1, waiting for transfers between devices, shards(): lax.all_gather(data_matrix, 'shot', axis=2, tiled=True)  222 us
    psum x1, waiting for transfers between devices, shards(): lax.psum(partial_terms.astype(jnp.bfloat16), 'rcv').astype(jnp.float32)  151 us
    dot_general x1, matrix products, complex_product(): jnp.einsum('afrk,bfks->abfrs', left, right, preferred_element_type=jnp.fl...  17.6 us
    unnamed x8, local copies, waits for them, and re-layouts  12 us
    psum x1, blocking collectives, shards(): sum_re, sum_im, sum_power = lax.psum((num_re, num_im, power), 'rcv')  10.3 us
  transfers between devices with their start and end apart: 2, of which 2 were waited for; matrix products, arithmetic and copies ran while one was open for 1% of the time, Pallas kernels for 0%

commit v1 on v0

--- a/solution.py
+++ b/solution.py
@@ -2,6 +2,11 @@
 import jax.numpy as jnp
 from jax import lax
 from jax.sharding import PartitionSpec as P
+
+
+def gather_and_add(x, axis):
+    parts = lax.all_gather(x, axis)
+    return jnp.sum(parts, axis=0)
 
 
 def complex_product(left, right):
@@ -15,7 +20,7 @@
     partial_terms = complex_product(
         lax.all_gather(data_matrix, "shot", axis=2, tiled=True), records
     )
-    summed = lax.psum(partial_terms.astype(jnp.bfloat16), "rcv").astype(jnp.float32)
+    summed = gather_and_add(partial_terms.astype(jnp.bfloat16), "rcv").astype(jnp.float32)
     total = lax.dynamic_slice_in_dim(summed, lax.axis_index("rcv") * own_rows, own_rows, 2)
     rec = records.astype(jnp.float32)
     num_re = jnp.sum(total[0] * rec[0] + total[1] * rec[1], axis=1)

time: 466 us -> 533 us (1.14)
  waiting for transfers between devices: 374 us -> 428 us
  other arithmetic: 38.4 us -> 49 us
    all_gather x0 -> x1, waiting for transfers between devices: none -> 200 us  [gather_and_add(): parts = lax.all_gather(x, axis)]
    psum x1 -> x0, waiting for transfers between devices: 151 us -> none  [shards(): lax.psum(partial_terms.astype(jnp.bfloat16), 'rcv').astype(jnp.float32)]
    reduce_sum x0 -> x1, other arithmetic: none -> 16.4 us  [gather_and_add(): return jnp.sum(parts, axis=0)]
    another operation x1 -> x2, other arithmetic: 3.84 us -> 19.6 us
    sub x1 -> x0, other arithmetic: 8.77 us -> none  [complex_product(): return jnp.stack((prod[0, 0] - prod[1, 1], prod[0, 1] + prod[1, 0]))]
    add x1 -> x0, other arithmetic: 6.6 us -> none  [complex_product(): return jnp.stack((prod[0, 0] - prod[1, 1], prod[0, 1] + prod[1, 0]))]
    unnamed x8 -> x10, local copies, waits for them, and re-layouts: 12 us -> 14.3 us
where the time goes in v1:
time: 533 us
  waiting for transfers between devices  428 us (80%)
  other arithmetic  49 us (9%)
  matrix products  17.6 us (3%)
  local copies, waits for them, and re-layouts  14.4 us (3%)
  between operations  14.1 us (3%)
  blocking collectives  10.3 us (2%)
    all_gather x1, waiting for transfers between devices, shards(): lax.all_gather(data_matrix, 'shot', axis=2, tiled=True)  228 us
    all_gather x1, waiting for transfers between devices, gather_and_add(): parts = lax.all_gather(x, axis)  200 us
    another operation x2, other arithmetic  19.6 us
    dot_general x1, matrix products, complex_product(): jnp.einsum('afrk,bfks->abfrs', left, right, preferred_element_type=jnp.fl...  17.6 us
    reduce_sum x1, other arithmetic, gather_and_add(): return jnp.sum(parts, axis=0)  16.4 us
    unnamed x10, local copies, waits for them, and re-layouts  14.3 us
  transfers between devices with their start and end apart: 2, of which 2 were waited for; matrix products, arithmetic and copies ran while one was open for 1% of the time, Pallas kernels for 0%

profile of v1, /device:TPU:0, one launch (start us, length us, event | category | flops | bytes accessed | tf_op | source)
XLA Modules:
  0.0 533.0 jit_solution(10698261718985932182)
XLA Ops:
  7.2 0.0 all-gather.3.cloned.1.call-start
  7.2 3.1 copy.9
  10.3 0.0 all-gather.3.cloned.1.call-update
  10.4 0.0 copy-start.2
  10.4 0.0 all-gather.5.cloned.1.call-start
  10.4 2.9 copy.8
  13.3 0.0 copy-done.2
  13.3 0.1 copy.7
  13.4 227.6 %all-gather.3.cloned.1.call-done = bf16[2,16,1024,256]{3,2,0,1:T(8,128)(2,1)} async-done(((bf16[2,16,128,256]{3,2,0,1:T(8,128)(2,1)}), bf16[2,16,1024,256]{3,2,0,1:T(8,128)(2,1)}) %all-gather.3.cloned.1.call-update) | async-done | bytes 16777232 | tf_op jit(solution)/shard_map/all_gather | solution.py:21
  241.1 17.6 %fusion.2 = f32[2,2,16,1024,128]{3,4,0,1,2:T(8,128)} fusion(bf16[2,16,1024,256]{3,2,0,1:T(8,128)(2,1)} %all-gather.3.cloned.1.call-done, bf16[2,16,256,128]{2,3,0,1:T(8,128)(2,1)S(1)} %copy.8, bf16[256,128]{0,1:T(8,128)(2,1)S(1)} %copy.7), kind=kOutput, calls=%fused_computation.2 | convolution fusion | flops 4299161600 | bytes 52494336 | tf_op jit(solution)/shard_map/afrk,bfks->abfrs/dot_general | solution.py:13
  258.7 15.7 %fusion.6 = (bf16[1,1,16,1024,128]{3,4,0,1,2:T(8,128)(2,1)}, bf16[1,1,16,1024,128]{3,4,0,1,2:T(8,128)(2,1)}) fusion(f32[2,2,16,1024,128]{3,4,0,1,2:T(8,128)} %fusion.2), kind=kLoop, calls=%fused_computation.6 | loop fusion | flops 8388608 | bytes 41943040 | tf_op jit(solution)/shard_map/convert.3
  274.4 7.4 %pad_maximum_fusion = bf16[1,2,16,1024,128]{3,4,0,1,2:T(8,128)(2,1)} fusion(bf16[1,1,16,1024,128]{3,4,0,1,2:T(8,128)(2,1)} %get-tuple-element.11, bf16[1,1,16,1024,128]{3,4,0,1,2:T(8,128)(2,1)} %get-tuple-element.10), kind=kLoop, calls=%fused_computation.7 | loop fusion | flops 4194304 | bytes 16777216 | tf_op jit(solution)/shard_map/stack | solution.py:14
  281.8 0.0 all-gather.5.cloned.1.call-update
  281.9 199.9 %all-gather.5.cloned.1.call-done = bf16[4,2,16,1024,128]{3,4,0,1,2:T(8,128)(2,1)} async-done(((bf16[1,2,16,1024,128]{3,4,0,1,2:T(8,128)(2,1)}), bf16[4,2,16,1024,128]{3,4,0,1,2:T(8,128)(2,1)}) %all-gather.5.cloned.1.call-update) | async-done | bytes 33554448 | tf_op jit(solution)/shard_map/all_gather | solution.py:8
  481.7 16.4 %reduce_sum.39 = bf16[2,16,1024,128]{2,3,0,1:T(8,128)(2,1)} reduce(bf16[4,2,16,1024,128]{3,4,0,1,2:T(8,128)(2,1)} %all-gather.5.cloned.1.call-done, bf16[]{:T(256)} %constant.5.clone.1), dimensions={0}, to_apply=%region_0.0 | reduce | flops 12582912 | bytes 41943040 | tf_op jit(solution)/shard_map/reduce_sum | solution.py:9
  498.1 4.2 dynamic-slice_convert_fusion
  502.3 0.0 copy-start
  502.3 0.0 copy-start.1
  502.3 1.2 add_reduce_fusion.1
  503.5 0.8 copy-done
  504.2 1.2 copy-done.1
  505.5 10.3 %all-reduce = (f32[16,128]{1,0:T(8,128)S(1)}, f32[16,128]{1,0:T(8,128)S(1)}, f32[16,128]{1,0:T(8,128)S(1)}) all-reduce(f32[16,128]{1,0:T(8,128)S(1)} %get-tuple-element.5, f32[16,128]{1,0:T(8,128)S(1)} %get-tuple-element.6, f32[16,128]{1,0:T(8,128)S(1)} %get-tuple-element.4), channel_id=1, replica_groups=mesh['shot'=8,'rcv'=4] {'rcv'}, use_global_device_ids=true, to_apply=%region_6.0 | all-reduce | flops 6144 | bytes 49152 | tf_op jit(solution)/shard_map/psum | solution.py:29
  515.8 3.9 subtract_convert_fusion.1
  519.7 0.2 pad_maximum_fusion.1
  519.9 2.4 copy.11
  522.3 3.9 copy.10
  (2 shorter events, 0.0 us)
Async XLA Ops:
  7.2 233.9 %all-gather.3.cloned.1.call-start = ((), (), s32[]{:S(2)}) async-start(), calls=%async_computation | async-start | bytes 18874368 | tf_op jit(solution)/shard_map/all_gather | solution.py:21
  10.4 2.9 copy-start.2
  10.4 471.3 %all-gather.5.cloned.1.call-start = ((), (), s32[]{:S(2)}) async-start(), calls=%async_computation.1 | async-start | bytes 41943040 | tf_op jit(solution)/shard_map/all_gather | solution.py:8
  502.3 2.0 copy-start
  502.3 3.2 copy-start.1
Sparse Core Ops, SparseCore 0:
  10.8 230.2 all-gather.2
  282.0 199.7 all-gather.4
